TPU v7x, 512 devices: a whole 4x8x8 slice. The times are simulated.
512 devices in a mesh: row: 16 (over y_hi, z), col: 32 (over y_lo, x, core).
Axes of the slice: x: 4, y: 8 (y_hi: 2, y_lo: 4; y = y_hi * 4 + y_lo), z: 8, core: 2. Of those that a mesh axis runs over, the one named last changes fastest.
Arguments:
- features: bfloat16 [65536, 256], P(('col', 'row')), may hold values from -6 to 6
- weight: bfloat16 [256, 256], replicated, may hold values from -0.375 to 0.375
- bias: float32 [256], replicated, may hold values from -3 to 3
- grad_out: bfloat16 [65536, 256], P(('row', 'col')), may hold values from -6 to 6
- tile_rows: int32 [16, 32, 128], P('row', 'col'), may hold values from 0 to 31
- tile_cols: int32 [16, 32, 128], P('row', 'col'), may hold values from 0 to 15
- tile_counts: int32 [16, 32], P('row', 'col'), may hold values from 1 to 128, as said below
- tile_values: bfloat16 [16, 32, 128, 128, 128], P('row', 'col'), may hold values from 0 to 0.011962891
Outputs:
- output: bfloat16 [65536, 256], P(('row', 'col'))
- grad_features: bfloat16 [65536, 256], P(('col', 'row'))
- grad_weight: float32 [256, 256], replicated
- grad_bias: float32 [256], replicated
Inputs may be any that keep to these rules, and one draw needn't show every extreme that they name: `tile_counts`: some grid cell has all 128 slots live. Tile coordinates may repeat within a cell; repeated tiles add.
All inputs are finite; a program needn't handle non-finite values.
Results may differ from a plain program's by a relative error of at most 0.018.
Values may be sent and summed in bfloat16 or wider, within the bound.
No kernel may reach another device: no remote copies, remote signals or barrier semaphores. Data moves between devices by JAX's collectives and lax.ppermute only.
A program may use at most 64 MiB of HBM per device.

v0:
```python
import jax
import jax.numpy as jnp
from jax import lax
from jax.sharding import PartitionSpec as P

GROUP = 8


def elu_value(pre):
    return jnp.where(pre > 0, pre, jnp.expm1(jnp.minimum(pre, 0.0)))


def elu_slope(pre):
    return jnp.where(pre > 0, jnp.float32(1.0), jnp.exp(jnp.minimum(pre, 0.0)))


def accumulate(values, dest_idx, src_idx, live, source, dest_tiles, transpose):
    side = values.shape[-1]
    width = source.shape[-1]
    group_size = GROUP
    blocks_all = source.reshape(source.shape[0] // side, side, width)

    def one_group(step, acc):
        first = step * group_size
        part_values = lax.dynamic_slice_in_dim(values, first, group_size, 0)
        part_dest = lax.dynamic_slice_in_dim(dest_idx, first, group_size, 0)
        part_src = lax.dynamic_slice_in_dim(src_idx, first, group_size, 0)
        blocks = jnp.take(blocks_all, part_src, axis=0)
        if transpose:
            prod = jnp.einsum(
                "gab,gac->gbc", part_values, blocks, preferred_element_type=jnp.float32
            )
        else:
            prod = jnp.einsum(
                "gab,gbc->gac", part_values, blocks, preferred_element_type=jnp.float32
            )
        keep = (jnp.arange(group_size) + first < live).astype(jnp.float32)
        return acc.at[part_dest].add(prod * keep[:, None, None])

    start_acc = jnp.zeros((dest_tiles, side, width), jnp.float32)
    steps_used = values.shape[0] // group_size
    total = lax.fori_loop(0, steps_used, one_group, start_acc)
    return total.reshape(dest_tiles * side, width)


def body(features, weight, bias, grad_out, tile_rows, tile_cols, tile_counts, tile_values):
    values = tile_values[0, 0]
    rows_idx = tile_rows[0, 0]
    cols_idx = tile_cols[0, 0]
    live = tile_counts[0, 0]
    side = values.shape[-1]
    share = features.shape[0]
    row_tiles = share * lax.axis_size("col") // side
    col_tiles = share * lax.axis_size("row") // side
    mixed = jnp.dot(features, weight, preferred_element_type=jnp.float32).astype(jnp.bfloat16)
    column_block = lax.all_gather(mixed, "row", axis=0, tiled=True)
    partial_value = accumulate(values, rows_idx, cols_idx, live, column_block, row_tiles, False)
    pre_share = (
        lax.psum_scatter(
            partial_value.astype(jnp.bfloat16), "col", scatter_dimension=0, tiled=True
        ).astype(jnp.float32)
        + bias[None, :]
    )
    grad_share = (grad_out.astype(jnp.float32) * elu_slope(pre_share)).astype(jnp.bfloat16)
    grad_block = lax.all_gather(grad_share, "col", axis=0, tiled=True)
    output = elu_value(pre_share).astype(jnp.bfloat16)
    back = accumulate(values, cols_idx, rows_idx, live, grad_block, col_tiles, True)
    grad_mixed = lax.psum_scatter(back.astype(jnp.bfloat16), "row", scatter_dimension=0, tiled=True)
    grad_features = lax.dot_general(
        grad_mixed, weight, (((1,), (1,)), ((), ())), preferred_element_type=jnp.float32
    ).astype(jnp.bfloat16)
    weight_term = lax.dot_general(
        features, grad_mixed, (((0,), (0,)), ((), ())), preferred_element_type=jnp.float32
    )
    bias_term = jnp.sum(grad_share.astype(jnp.float32), axis=0)
    grad_weight, grad_bias = lax.psum((weight_term, bias_term), ("row", "col"))
    return (output, grad_features, grad_weight, grad_bias)


def solution(mesh):
    placed = (
        P(("col", "row"), None),
        P(),
        P(),
        P(("row", "col"), None),
        P("row", "col", None),
        P("row", "col", None),
        P("row", "col"),
        P("row", "col", None, None, None),
    )
    return jax.shard_map(
        body,
        mesh=mesh,
        in_specs=placed,
        out_specs=(P(("row", "col"), None), P(("col", "row"), None), P(), P()),
        check_vma=False,
    )
```

profile of v0, /device:TPU:23, one launch (start us, length us, event | category | flops | bytes accessed | tf_op | source)
XLA Modules:
  0.0 1037.7 jit_solution(1046019565683276147)
XLA Ops:
  9.8 93.5 %all-gather.3.cloned.1.call-done = bf16[2048,256]{1,0:T(8,128)(2,1)} async-done(((bf16[128,256]{1,0:T(8,128)(2,1)}), bf16[2048,256]{1,0:T(8,128)(2,1)}) %all-gather.3.cloned.1.call-update) | async-done | bytes 1048592 | tf_op jit(solution)/shard_map/all_gather | solution.py:56
  105.7 96.6 %while.26 = (s32[]{:T(128)}, f32[32,128,256]{2,1,0:T(8,128)}, s32[128]{0:T(128)S(1)}, bf16[128,128,128]{2,1,0:T(8,128)(2,1)}, s32[128]{0:T(128)S(1)}, /*index=5*...) while((s32[]{:T(128)}, f32[32,128,256]{2,1,0:T(8,128)}, ...), condition=%wide.region_2.3_spmd, body=%wide.region_0.2_spmd.sunk | while | flops 67896424 | bytes 6033887 | solution.py:42
  108.4 3.3 scatter_fusion
  114.5 3.3 scatter_fusion
  120.6 3.3 scatter_fusion
  150.6 3.3 scatter_fusion
  162.7 3.3 scatter_fusion
  174.7 3.3 scatter_fusion
  186.8 3.4 scatter_fusion
  192.9 3.4 scatter_fusion
  202.3 3.8 convert_element_type.56
  206.2 125.6 %reduce-scatter.3.cloned.1.call-done = bf16[128,256]{1,0:T(8,128)(2,1)} async-done(((bf16[4096,256]{1,0:T(8,128)(2,1)}), bf16[128,256]{1,0:T(8,128)(2,1)}) %reduce-scatter.3.cloned.1.call-update) | async-done | bytes 65552 | tf_op jit(solution)/shard_map/reduce_scatter | solution.py:59
  333.5 6.4 copy.12
  339.9 75.5 %all-gather.5.cloned.1.call-done = bf16[4096,256]{1,0:T(8,128)(2,1)} async-done(((bf16[128,256]{1,0:T(8,128)(2,1)}), bf16[4096,256]{1,0:T(8,128)(2,1)}) %all-gather.5.cloned.1.call-update) | async-done | bytes 2097168 | tf_op jit(solution)/shard_map/all_gather | solution.py:65
  417.0 121.8 %while.27 = (s32[]{:T(128)}, f32[16,128,256]{2,1,0:T(8,128)}, s32[128]{0:T(128)S(1)}, bf16[128,128,128]{1,2,0:T(8,128)(2,1)}, s32[128]{0:T(128)S(1)}, /*index=5*...) while((s32[]{:T(128)}, f32[16,128,256]{2,1,0:T(8,128)}, ...), condition=%wide.region_6.7_spmd, body=%wide.region_4.6_spmd.sunk | while | flops 67896424 | bytes 6033887 | solution.py:42
  428.9 3.3 scatter_fusion.1
  444.2 3.3 scatter_fusion.1
  474.6 3.3 scatter_fusion.1
  489.9 3.3 scatter_fusion.1
  505.1 3.3 scatter_fusion.1
  520.3 3.3 scatter_fusion.1
  541.6 97.9 %psum.15 = f32[256]{0:T(256)} all-reduce(f32[256]{0:T(256)S(1)} %get-tuple-element.297), channel_id=1, replica_groups=mesh['row'=16,'col'=32] {'row','col'}, use_global_device_ids=true, to_apply=%region_10.11 | all-reduce | flops 256 | bytes 2048 | tf_op jit(solution)/shard_map/psum | solution.py:76
  639.5 113.2 %reduce-scatter.5.cloned.1.call-done = bf16[128,256]{1,0:T(8,128)(2,1)} async-done(((bf16[2048,256]{1,0:T(8,128)(2,1)}), bf16[128,256]{1,0:T(8,128)(2,1)}) %reduce-scatter.5.cloned.1.call-update) | async-done | bytes 65552 | tf_op jit(solution)/shard_map/reduce_scatter | solution.py:68
  756.2 273.2 %all-reduce.2.cloned.1.call-done = f32[256,256]{0,1:T(8,128)} async-done(((f32[256,256]{0,1:T(8,128)}), f32[256,256]{0,1:T(8,128)}) %all-reduce.2.cloned.1.call-update) | async-done | bytes 262160 | tf_op jit(solution)/shard_map/psum | solution.py:76
  (210 shorter events, 187.5 us)
Async XLA Ops:
  7.2 0.9 copy-start
  7.2 98.5 %copy-start.4 = (s32[1,1,128]{2,1,0:T(1,128)S(1)}, s32[1,1,128]{2,1,0:T(1,128)}, u32[]{:S(2)}) copy-start(s32[1,1,128]{2,1,0:T(1,128)} %param.16) | copy-start | bytes 1540
  7.2 98.5 %copy-start.5 = (s32[1,1,128]{2,1,0:T(1,128)S(1)}, s32[1,1,128]{2,1,0:T(1,128)}, u32[]{:S(2)}) copy-start(s32[1,1,128]{2,1,0:T(1,128)} %param.17) | copy-start | bytes 1540
  7.2 96.1 %all-gather.3.cloned.1.call-start = ((), (), s32[]{:S(2)}) async-start(), calls=%async_computation.2 | async-start | bytes 1114112 | tf_op jit(solution)/shard_map/all_gather | solution.py:56
  9.7 322.1 %reduce-scatter.3.cloned.1.call-start = ((), (), s32[]{:S(2)}) async-start(), calls=%async_computation.3 | async-start | bytes 2162688 | tf_op jit(solution)/shard_map/reduce_scatter | solution.py:59
  103.3 2.4 copy-start.1
  202.3 129.6 %copy-start.3 = (bf16[128,256]{1,0:T(8,128)(2,1)S(1)}, bf16[128,256]{1,0:T(8,128)(2,1)}, u32[]{:S(2)}) copy-start(bf16[128,256]{1,0:T(8,128)(2,1)} %param.15) | copy-start | bytes 196612
  202.3 129.6 %copy-start.6 = (f32[256]{0:T(256)S(1)}, f32[256]{0:T(256)}, u32[]{:S(2)}) copy-start(f32[256]{0:T(256)} %param.14) | copy-start | bytes 3076
  206.1 209.3 %all-gather.5.cloned.1.call-start = ((), (), s32[]{:S(2)}) async-start(), calls=%async_computation.4 | async-start | bytes 2162688 | tf_op jit(solution)/shard_map/all_gather | solution.py:65
  333.4 419.3 %reduce-scatter.5.cloned.1.call-start = ((), (), s32[]{:S(2)}) async-start(), calls=%async_computation.5 | async-start | bytes 1114112 | tf_op jit(solution)/shard_map/reduce_scatter | solution.py:68
  538.8 213.9 %copy-start.2 = (bf16[128,256]{1,0:T(8,128)(2,1)S(1)}, bf16[128,256]{1,0:T(8,128)(2,1)}, u32[]{:S(2)}) copy-start(bf16[128,256]{1,0:T(8,128)(2,1)} %param.12) | copy-start | bytes 196612
  541.6 487.8 %all-reduce.2.cloned.1.call-start = ((), (), s32[]{:S(2)}) async-start(), calls=%async_computation.6 | async-start | bytes 524288 | tf_op jit(solution)/shard_map/psum | solution.py:76
Sparse Core Ops, SparseCore 0:
  11.8 91.4 all-gather.2
  206.3 125.5 reduce-scatter.2
  334.8 80.5 all-gather.4
  541.7 210.9 reduce-scatter.4
  758.9 270.4 all-reduce.1
where the time goes:
time: 1040 us
  waiting for transfers between devices  681 us (65%)
  other arithmetic  140 us (13%)
  blocking collectives  97.9 us (9%)
  local copies, waits for them, and re-layouts  57 us (5%)
  matrix products  47.3 us (5%)
  between operations  13.8 us (1%)
    psum x1, waiting for transfers between devices, body(): grad_weight, grad_bias = lax.psum((weight_term, bias_term), ('row', 'col'))  273 us
    reduce_scatter x1, waiting for transfers between devices, body(): lax.psum_scatter(partial_value.astype(jnp.bfloat16), 'col', scatter_dimen...  126 us
    reduce_scatter x1, waiting for transfers between devices, body(): lax.psum_scatter(back.astype(jnp.bfloat16), 'row', scatter_dimension=0, t...  113 us
    scatter-add x32, other arithmetic, one_group(): return acc.at[part_dest].add(prod * keep[:, None, None])  106 us
    psum x1, blocking collectives, body(): grad_weight, grad_bias = lax.psum((weight_term, bias_term), ('row', 'col'))  97.9 us
    all_gather x1, waiting for transfers between devices, body(): column_block = lax.all_gather(mixed, 'row', axis=0, tiled=True)  93.5 us
    all_gather x1, waiting for transfers between devices, body(): grad_block = lax.all_gather(grad_share, 'col', axis=0, tiled=True)  75.5 us
    gather x32, local copies, waits for them, and re-layouts, one_group(): blocks = jnp.take(blocks_all, part_src, axis=0)  44 us
  transfers between devices with their start and end apart: 5, of which 5 were waited for; matrix products, arithmetic and copies ran while one was open for 1% of the time, Pallas kernels for 0%

commit v1 on v0

--- a/solution.py
+++ b/solution.py
@@ -2,6 +2,7 @@
 import jax.numpy as jnp
 from jax import lax
 from jax.sharding import PartitionSpec as P
+from jax.lax import psum
 
 GROUP = 8
 
@@ -73,7 +74,15 @@
         features, grad_mixed, (((0,), (0,)), ((), ())), preferred_element_type=jnp.float32
     )
     bias_term = jnp.sum(grad_share.astype(jnp.float32), axis=0)
-    grad_weight, grad_bias = lax.psum((weight_term, bias_term), ("row", "col"))
+
+    def choose_slot_up(v0):
+        comm_axis = "col"
+        group_axis = "row"
+        for s in (group_axis, comm_axis):
+            v0 = psum(v0, s)
+        return v0
+
+    grad_weight, grad_bias = choose_slot_up((weight_term, bias_term))
     return (output, grad_features, grad_weight, grad_bias)
 
 

time: 1040 us -> 1250 us (1.20)
  the two profiles are of different devices: /device:TPU:23 before, /device:TPU:1 now
where the time goes in v1:
time: 1250 us; the launch traced here: 1240 us
  waiting for transfers between devices  852 us (68%)
  other arithmetic  139 us (11%)
  blocking collectives  132 us (11%)
  local copies, waits for them, and re-layouts  57 us (5%)
  matrix products  47.3 us (4%)
  between operations  14.1 us (1%)
    psum x2, waiting for transfers between devices, choose_slot_up(): v0 = psum(v0, s)  343 us
    reduce_scatter x1, waiting for transfers between devices, body(): lax.psum_scatter(back.astype(jnp.bfloat16), 'row', scatter_dimension=0, t...  211 us
    reduce_scatter x1, waiting for transfers between devices, body(): lax.psum_scatter(partial_value.astype(jnp.bfloat16), 'col', scatter_dimen...  146 us
    psum x2, blocking collectives, choose_slot_up(): v0 = psum(v0, s)  132 us
    scatter-add x32, other arithmetic, one_group(): return acc.at[part_dest].add(prod * keep[:, None, None])  105 us
    all_gather x1, waiting for transfers between devices, body(): column_block = lax.all_gather(mixed, 'row', axis=0, tiled=True)  92.8 us
    all_gather x1, waiting for transfers between devices, body(): grad_block = lax.all_gather(grad_share, 'col', axis=0, tiled=True)  58.6 us
    gather x32, local copies, waits for them, and re-layouts, one_group(): blocks = jnp.take(blocks_all, part_src, axis=0)  44 us
  transfers between devices with their start and end apart: 6, of which 6 were waited for; matrix products, arithmetic and copies ran while one was open for 1% of the time, Pallas kernels for 0%

profile of v1, /device:TPU:1, one launch (start us, length us, event | category | flops | bytes accessed | tf_op | source)
XLA Modules:
  0.0 1242.3 jit_solution(4216942000139549076)
XLA Ops:
  9.8 92.8 %all-gather.3.cloned.1.call-done = bf16[2048,256]{1,0:T(8,128)(2,1)} async-done(((bf16[128,256]{1,0:T(8,128)(2,1)}), bf16[2048,256]{1,0:T(8,128)(2,1)}) %all-gather.3.cloned.1.call-update) | async-done | bytes 1048592 | tf_op jit(solution)/shard_map/all_gather | solution.py:57
  105.0 96.4 %while.26 = (s32[]{:T(128)}, f32[32,128,256]{2,1,0:T(8,128)}, s32[128]{0:T(128)S(1)}, bf16[128,128,128]{2,1,0:T(8,128)(2,1)}, s32[128]{0:T(128)S(1)}, /*index=5*...) while((s32[]{:T(128)}, f32[32,128,256]{2,1,0:T(8,128)}, ...), condition=%wide.region_2.3_spmd, body=%wide.region_0.2_spmd.sunk | while | flops 67896424 | bytes 6033887 | solution.py:43
  113.8 3.3 scatter_fusion
  119.8 3.3 scatter_fusion
  125.9 3.3 scatter_fusion
  131.9 3.3 scatter_fusion
  138.0 3.3 scatter_fusion
  150.0 3.3 scatter_fusion
  201.4 3.8 convert_element_type.56
  205.3 146.1 %reduce-scatter.3.cloned.1.call-done = bf16[128,256]{1,0:T(8,128)(2,1)} async-done(((bf16[4096,256]{1,0:T(8,128)(2,1)}), bf16[128,256]{1,0:T(8,128)(2,1)}) %reduce-scatter.3.cloned.1.call-update) | async-done | bytes 65552 | tf_op jit(solution)/shard_map/reduce_scatter | solution.py:60
  353.1 6.4 copy.12
  359.5 58.6 %all-gather.5.cloned.1.call-done = bf16[4096,256]{1,0:T(8,128)(2,1)} async-done(((bf16[128,256]{1,0:T(8,128)(2,1)}), bf16[4096,256]{1,0:T(8,128)(2,1)}) %all-gather.5.cloned.1.call-update) | async-done | bytes 2097168 | tf_op jit(solution)/shard_map/all_gather | solution.py:66
  419.7 121.8 %while.27 = (s32[]{:T(128)}, f32[16,128,256]{2,1,0:T(8,128)}, s32[128]{0:T(128)S(1)}, bf16[128,128,128]{1,2,0:T(8,128)(2,1)}, s32[128]{0:T(128)S(1)}, /*index=5*...) while((s32[]{:T(128)}, f32[16,128,256]{2,1,0:T(8,128)}, ...), condition=%wide.region_6.7_spmd, body=%wide.region_4.6_spmd.sunk | while | flops 67896424 | bytes 6033887 | solution.py:43
  431.6 3.3 scatter_fusion.1
  439.2 3.3 scatter_fusion.1
  446.9 3.3 scatter_fusion.1
  462.1 3.3 scatter_fusion.1
  469.8 3.3 scatter_fusion.1
  530.5 3.3 scatter_fusion.1
  544.2 211.2 %reduce-scatter.5.cloned.1.call-done = bf16[128,256]{1,0:T(8,128)(2,1)} async-done(((bf16[2048,256]{1,0:T(8,128)(2,1)}), bf16[128,256]{1,0:T(8,128)(2,1)}) %reduce-scatter.5.cloned.1.call-update) | async-done | bytes 65552 | tf_op jit(solution)/shard_map/reduce_scatter | solution.py:69
  757.3 186.7 %all-reduce.3.cloned.1.call-done = f32[256,256]{0,1:T(8,128)} async-done(((f32[256,256]{0,1:T(8,128)}), f32[256,256]{0,1:T(8,128)}) %all-reduce.3.cloned.1.call-update) | async-done | bytes 262160 | tf_op jit(solution)/shard_map/psum | solution.py:82
  944.0 45.7 %psum.30 = f32[256]{0:T(256)S(1)} all-reduce(f32[256]{0:T(256)S(1)} %get-tuple-element.297), channel_id=1, replica_groups=mesh['row'=16,'col'=32] {'row'}, use_global_device_ids=true, to_apply=%region_11.12 | all-reduce | flops 256 | bytes 2048 | tf_op jit(solution)/shard_map/psum | solution.py:82
  989.7 85.9 %psum.31 = f32[256]{0:T(256)} all-reduce(f32[256]{0:T(256)S(1)} %psum.30), channel_id=1, replica_groups=mesh['row'=16,'col'=32] {'col'}, use_global_device_ids=true, to_apply=%region_12.13 | all-reduce | flops 256 | bytes 2048 | tf_op jit(solution)/shard_map/psum | solution.py:82
  1077.3 156.4 %all-reduce.5.cloned.1.call-done = f32[256,256]{0,1:T(8,128)} async-done(((f32[256,256]{0,1:T(8,128)}), f32[256,256]{0,1:T(8,128)}) %all-reduce.5.cloned.1.call-update) | async-done | bytes 262160 | tf_op jit(solution)/shard_map/psum | solution.py:82
  (214 shorter events, 194.0 us)
Async XLA Ops:
  7.2 0.9 copy-start
  7.2 97.8 %copy-start.4 = (s32[1,1,128]{2,1,0:T(1,128)S(1)}, s32[1,1,128]{2,1,0:T(1,128)}, u32[]{:S(2)}) copy-start(s32[1,1,128]{2,1,0:T(1,128)} %param.16) | copy-start | bytes 1540
  7.2 97.8 %copy-start.5 = (s32[1,1,128]{2,1,0:T(1,128)S(1)}, s32[1,1,128]{2,1,0:T(1,128)}, u32[]{:S(2)}) copy-start(s32[1,1,128]{2,1,0:T(1,128)} %param.17) | copy-start | bytes 1540
  7.2 95.3 %all-gather.3.cloned.1.call-start = ((), (), s32[]{:S(2)}) async-start(), calls=%async_computation.2 | async-start | bytes 1114112 | tf_op jit(solution)/shard_map/all_gather | solution.py:57
  9.7 341.7 %reduce-scatter.3.cloned.1.call-start = ((), (), s32[]{:S(2)}) async-start(), calls=%async_computation.3 | async-start | bytes 2162688 | tf_op jit(solution)/shard_map/reduce_scatter | solution.py:60
  102.5 2.4 copy-start.1
  201.4 150.0 %copy-start.3 = (bf16[128,256]{1,0:T(8,128)(2,1)S(1)}, bf16[128,256]{1,0:T(8,128)(2,1)}, u32[]{:S(2)}) copy-start(bf16[128,256]{1,0:T(8,128)(2,1)} %param.15) | copy-start | bytes 196612
  201.4 150.0 %copy-start.6 = (f32[256]{0:T(256)S(1)}, f32[256]{0:T(256)}, u32[]{:S(2)}) copy-start(f32[256]{0:T(256)} %param.14) | copy-start | bytes 3076
  205.3 212.9 %all-gather.5.cloned.1.call-start = ((), (), s32[]{:S(2)}) async-start(), calls=%async_computation.4 | async-start | bytes 2162688 | tf_op jit(solution)/shard_map/all_gather | solution.py:66
  353.1 402.4 %reduce-scatter.5.cloned.1.call-start = ((), (), s32[]{:S(2)}) async-start(), calls=%async_computation.5 | async-start | bytes 1114112 | tf_op jit(solution)/shard_map/reduce_scatter | solution.py:69
  541.5 214.0 %copy-start.2 = (bf16[128,256]{1,0:T(8,128)(2,1)S(1)}, bf16[128,256]{1,0:T(8,128)(2,1)}, u32[]{:S(2)}) copy-start(bf16[128,256]{1,0:T(8,128)(2,1)} %param.12) | copy-start | bytes 196612
  544.2 399.8 %all-reduce.3.cloned.1.call-start = ((), (), s32[]{:S(2)}) async-start(), calls=%async_computation.6 | async-start | bytes 524288 | tf_op jit(solution)/shard_map/psum | solution.py:82
  757.2 476.5 %all-reduce.5.cloned.1.call-start = ((), (), s32[]{:S(2)}) async-start(), calls=%async_computation.7 | async-start | bytes 524288 | tf_op jit(solution)/shard_map/psum | solution.py:82
Sparse Core Ops, SparseCore 0:
  11.8 90.7 all-gather.2
  205.4 146.0 reduce-scatter.2
  354.4 63.6 all-gather.4
  544.3 211.0 reduce-scatter.4
  759.0 184.9 all-reduce.2
  946.7 286.9 all-reduce.4
